TPU v7x, 32 devices: a whole 2x2x4 slice. The times are simulated.
32 devices in a mesh: dp: 4 (over z), context: 2 (over core), tensor: 4 (over y, x).
Axes of the slice: x: 2, y: 2, z: 4, core: 2. Of those that a mesh axis runs over, the one named last changes fastest.
Arguments:
- tokens: bfloat16 [12, 2048, 768], P('dp', ('context', 'tensor')), may hold values from -6 to 6
- segments: int32 [12, 2048], P('dp'), may hold values from 0 to 7, never falling along the last dimension, each value on 1 to 1792 neighbouring positions
- w_qkv: bfloat16 [768, 3, 768], P('dp', None, 'tensor'), may hold values from -0.21875 to 0.21875
- w_out: bfloat16 [768, 768], P('tensor', 'dp'), may hold values from -1.5 to 1.5
- w_in: bfloat16 [768, 3072], P('dp', 'tensor'), may hold values from -0.21875 to 0.21875
- w_back: bfloat16 [3072, 768], P('tensor', 'dp'), may hold values from -0.109375 to 0.109375
- gain_attn: bfloat16 [768], P('dp'), may hold values from 0.25 to 1.75
- gain_mlp: bfloat16 [768], P('dp'), may hold values from 0.25 to 1.75
- cotangent: bfloat16 [12, 2048, 768], P('dp', ('context', 'tensor')), may hold values from -6 to 6
Outputs:
- output: bfloat16 [12, 2048, 768], P('dp', ('context', 'tensor'))
- grad_tokens: bfloat16 [12, 2048, 768], P('dp', ('context', 'tensor'))
- grad_w_qkv: float32 [768, 3, 768], P('dp', None, 'tensor')
- grad_w_out: float32 [768, 768], P('tensor', 'dp')
- grad_w_in: float32 [768, 3072], P('dp', 'tensor')
- grad_w_back: float32 [3072, 768], P('tensor', 'dp')
- grad_gain_attn: float32 [768], P('dp')
- grad_gain_mlp: float32 [768], P('dp')
Inputs may be any that keep to these rules, and one draw needn't show every extreme that they name: `segments`: within a sequence the numbers never fall; a document holds 1 to 1792 bytes, and some document holds exactly 1792.
All inputs are finite; a program needn't handle non-finite values.
Results may differ from a plain program's by a relative error of at most 0.02.
Values may be sent and summed in bfloat16 or wider, within the bound.
A program may use at most 192 MiB of HBM per device.

v0:
```python
import functools
import math

import jax
import jax.numpy as jnp
from jax import lax
from jax.experimental import pallas as pl
from jax.experimental.pallas import tpu as pltpu
from jax.sharding import PartitionSpec as P

HD = 64
WIN = 1536
QB = 256
CHUNK = 128
NEG = -1e30
epsilon = 1e-06
low = jnp.bfloat16
full = jnp.float32


def dot(left, right, dims):
    return lax.dot_general(left, right, (dims, ((), ())), preferred_element_type=full)


def nn(left, right):
    return dot(left, right, ((1,), (0,)))


def nt(left, right):
    return dot(left, right, ((1,), (1,)))


def tn(left, right):
    return dot(left, right, ((0,), (0,)))


PEERS = [(dc, r) for dc in range(2) for r in range(4)]


def place():
    return lax.axis_index("context"), lax.axis_index("tensor")


def at_peer(c, t, dc, r):
    return {"context": c ^ dc, "tensor": t ^ r}


def greet(peers):
    for peer in peers:
        pl.semaphore_signal(pltpu.get_barrier_semaphore(), inc=1, device_id=peer)


def greeted(peers):
    pl.semaphore_wait(pltpu.get_barrier_semaphore(), len(peers))


def unit_place(u, c):
    return jnp.where(u < 3, u, c + u - 3), jnp.where(u < 3, 2 * c, 1)


def sends(u, c):
    return (u != 3) | (c == 0)


dma = pltpu.SemaphoreType.DMA
ANY = pl.BlockSpec(memory_space=pl.ANY)
VMEM = pl.BlockSpec(memory_space=pltpu.VMEM)
HBM = pl.BlockSpec(memory_space=pltpu.HBM)
shape = jax.ShapeDtypeStruct

SIDE = 128


class Line:
    def __init__(self, n, own, slot, send, recv):
        self.n, self.own, self.slot, self.sems = n, own, slot, (send, recv)
        self.d = lax.axis_index("dp")

    def along(self, k):
        m = self.d if k == 0 else self.n - 1 - self.d
        to = {"dp": jnp.clip(self.d + 1 if k == 0 else self.d - 1, 0, self.n - 1)}
        return m, to

    def target(self, k, step):
        m, _ = self.along(k)
        return jnp.clip(self.n - step + m if k == 0 else step - 1 - m, 0, self.n - 1)

    def copy(self, k, step, src):
        send, recv = self.sems
        _, to = self.along(k)
        return pltpu.make_async_remote_copy(
            src, self.slot(k, step), send.at[k, step - 1], recv.at[k, step - 1], device_id=to
        )

    def arrive(self, k, step):
        self.copy(k, step, self.slot(k, step)).wait_recv()

    def start(self, step, add):
        for k in range(2):
            m, _ = self.along(k)
            if step > 1:

                @pl.when((m >= 1) & (m < self.n - 1) & (step >= m + 1))
                def _():
                    add(k, self.target(k, step))
                    self.copy(k, step, self.slot(k, step - 1)).start()

            @pl.when(m == 0)
            def _():
                self.copy(k, step, self.own(self.target(k, step))).start()

    def received(self, step):
        for k in range(2):
            m, _ = self.along(k)

            @pl.when((m >= 1) & (step >= m))
            def _():
                self.arrive(k, step)

    def sent(self, step):
        for k in range(2):
            m, _ = self.along(k)

            @pl.when((m < self.n - 1) & (step >= m + 1))
            def _():
                self.copy(k, step, self.slot(k, step)).wait_send()


def greet_line(n, d):
    barrier = pltpu.get_barrier_semaphore()

    @pl.when(d > 0)
    def _():
        pl.semaphore_signal(barrier, inc=1, device_id={"dp": jnp.maximum(d - 1, 0)})

    @pl.when(d < n - 1)
    def _():
        pl.semaphore_signal(barrier, inc=1, device_id={"dp": jnp.minimum(d + 1, n - 1)})


def greeted_line(n, d, peers):
    ends = jnp.where(d > 0, 1, 0) + jnp.where(d < n - 1, 1, 0)
    pl.semaphore_wait(pltpu.get_barrier_semaphore(), len(peers) + ends)


def project_kernel(
    n, tokens, segments, w_qkv, up, out_own, gain_one, gain_two, qkv, norm, w_t, up_all, out_all, gain_ref, lo_ref,
    tok, x, w, proj, out_w, gain, own_gain, tsend, trecv, tlocal, wsend, wrecv, wlocal, osend, orecv, olocal, xsend, xrecv,
):
    c, t = place()
    d = lax.axis_index("dp")
    own = tokens.shape[1]
    width = tokens.shape[2]
    span = 4 * own
    shard = up.shape[0]
    half = own // 2
    hidden = up_all.shape[1]
    cut = n // 2
    to_x, to_y, to_core = {"tensor": t ^ 1}, {"tensor": t ^ 2}, {"context": 1 - c}
    others = [{"dp": lax.rem(d + r, n)} for r in range(1, n)]
    peers = [to_x, to_y, to_core] + others
    greet(peers)

    def local(i, s):
        return pltpu.make_async_copy(tokens.at[s], tok.at[s, t], tlocal.at[i])

    def weights(j, r):
        rows = pl.ds(pl.multiple_of(d * shard, shard), shard)
        source, target = (
            (w_qkv, w.at[:, rows]),
            (out_w, out_all.at[rows]),
            (up.at[:, pl.ds(pl.multiple_of(c * hidden, hidden), hidden)], up_all.at[rows]),
            (own_gain, gain.at[d]),
        )[j]
        if r == 0:
            return pltpu.make_async_copy(source, target, wlocal.at[j])
        return pltpu.make_async_remote_copy(
            source, target, wsend.at[j, r - 1], wrecv.at[j, r - 1], device_id=others[r - 1]
        )

    def gives(j, r):
        return lax.rem(d + n - r, n) // cut == c if j < 2 else True

    def weights_do(j, r, what, source=False):
        @pl.when(gives(j, 0 if source else r))
        def _():
            getattr(weights(j, r), what)()

    def to_other(j):
        rows = pl.ds(pl.multiple_of(c * cut * shard, shard), cut * shard)
        ref = w.at[:, rows]
        return pltpu.make_async_remote_copy(ref, ref, xsend, xrecv, device_id=to_core)

    order = (2 * (1 - c), 1, 2 * c)
    for i, s in enumerate(order):
        local(i, s).start()
    out_w[...] = out_own[...].T
    own_gain[...] = jnp.zeros_like(own_gain)
    own_gain[0:1, :] = gain_one[...]
    own_gain[1:2, :] = gain_two[...]
    for j in range(4):
        weights_do(j, 0, "start")
    greeted(peers)
    for j in (0, 3, 1, 2):
        for r in range(1, n):
            weights_do(j, r, "start", True)

    def hop(k, i):
        s = order[i]
        origin, rows, peer = (
            (t, slice(0, half), to_x),
            (t, slice(half, own), to_y),
            (t, slice(0, half), to_y),
            (t, slice(half, own), to_x),
            (t ^ 1, slice(0, half), to_y),
            (t ^ 2, slice(half, own), to_x),
        )[k]
        there = tok.at[s, origin, rows]
        here = tokens.at[s, rows] if k < 4 else there
        return pltpu.make_async_remote_copy(
            here, there, tsend.at[k, i], trecv.at[k, i], device_id=peer
        )

    def straight(i):
        for k in range(4):
            hop(k, i).start()

    def forward(i):
        for k in range(2):
            hop(k, i).wait_recv()
            hop(k + 4, i).start()

    units = proj.shape[1]

    def leave(i):
        out = []
        lanes = pl.ds(pl.multiple_of(c * span, span), span)
        if i != 0:
            out.append((x.at[i], norm.at[2 - i, lanes], False))
        if i != 2:
            out.append((x.at[i], norm.at[i, lanes], True))
        if i == 0:
            out.append((proj.at[0], qkv.at[pl.ds(0, units), :, lanes], True))
        if i == 2:
            out.append((proj.at[2], qkv.at[pl.ds(0, units), :, lanes], False))
        if i == 1:
            for away in (True, False):
                core = 1 - c if away else c
                for p in range(3):
                    src = proj.at[1, pl.ds(p * 3 + core, 2)]
                    out.append((src, qkv.at[pl.ds(units + 2 * p, 2), :, lanes], away))
        copies = []
        for j, (src, dst, away) in enumerate(out):
            if away:
                copies.append(
                    (away, pltpu.make_async_remote_copy(src, dst, osend.at[i, j], orecv.at[i, j], device_id=to_core))
                )
            else:
                copies.append((away, pltpu.make_async_copy(src, dst, olocal.at[i, j])))
        return copies

    def work(i):
        s = order[i]
        local(i, s).wait()
        for k in range(2, 6):
            hop(k, i).wait_recv()

        @pl.loop(0, 4)
        def _(p):
            rows = pl.ds(pl.multiple_of(p * own, own), own)
            v = tok[s, p].astype(full)
            inv = lax.rsqrt(jnp.mean(v * v, axis=-1, keepdims=True) + epsilon)
            normed = (v * inv * gain_ref[0:1, :]).astype(low)
            x[i, rows, :] = normed
            proj[i, :, :, rows] = nt(w_t[...], normed).astype(low).reshape(units, HD, own)

        for _, copy in leave(i):
            copy.start()

    straight(0)
    straight(1)
    forward(0)
    straight(2)
    seg = segments[...]
    first = jnp.zeros(seg.shape, jnp.int32)
    for value in range(8):
        before = jnp.sum((seg < value).astype(jnp.int32), axis=1, keepdims=True)
        first = jnp.where(seg == value, before, first)
    first = jnp.maximum(first, lax.broadcasted_iota(jnp.int32, seg.shape, 1) - (WIN - 1))
    lo_ref[0] = jnp.where(c == 0, first[0:1], first[2:3])
    lo_ref[1] = first[1:2]
    weights_do(0, 0, "wait")
    for r in range(1, n):
        weights_do(0, r, "wait_recv")
    to_other(0).start()
    weights(3, 0).wait()
    for r in range(1, n):
        weights(3, r).wait_recv()
    gain_ref[...] = jnp.concatenate([gain[i].astype(full) for i in range(n)], axis=1)[:8]
    to_other(0).wait_recv()
    for p in range(3):
        w_t[p * 3 * HD : (p + 1) * 3 * HD, :] = w[p].T
    forward(1)
    work(0)
    forward(2)
    work(1)
    work(2)
    to_other(0).wait_send()
    for j in range(4):
        if j in (1, 2):
            weights_do(j, 0, "wait")
        for r in range(1, n):
            weights_do(j, r, "wait_send", True)
            if j in (1, 2):
                weights_do(j, r, "wait_recv")
    for i in range(3):
        for k in range(6):
            hop(k, i).wait_send()
        for away, copy in leave(i):
            copy.wait()


def project(n, tokens, segments, w_qkv, up, out_own, gain_one, gain_two):
    sequences, own, width = tokens.shape
    shard, hidden = up.shape[0], up.shape[1] // 2
    local = out_own.shape[0]
    span = 4 * own
    return pl.pallas_call(
        functools.partial(project_kernel, n),
        in_specs=[HBM, VMEM, HBM, HBM, VMEM, VMEM, VMEM],
        out_specs=[HBM] * 2 + [VMEM] + [HBM] * 2 + [VMEM] * 2,
        out_shape=[
            shape((15, HD, 2 * span), low),
            shape((2, 2 * span, width), low),
            shape((9 * HD, n * shard), low),
            shape((n * shard, hidden), low),
            shape((n * shard, local), low),
            shape((8, n * shard), full),
            shape((2, 1, segments.shape[1]), jnp.int32),
        ],
        scratch_shapes=[
            pltpu.VMEM((sequences, 4, own, width), low),
            pltpu.VMEM((sequences, span, width), low),
            pltpu.VMEM((3, n * shard, local), low),
            pltpu.VMEM((sequences, 9, HD, span), low),
            pltpu.VMEM((shard, local), low),
            pltpu.VMEM((n, 16, shard), low),
            pltpu.VMEM((16, shard), low),
            dma((6, 3)), dma((6, 3)), dma((3,)),
            dma((4, n - 1)), dma((4, n - 1)), dma((4,)),
            dma((3, 8)), dma((3, 8)), dma((3, 8)), dma, dma,
        ],
        compiler_params=pltpu.CompilerParams(
            vmem_limit_bytes=63 << 20, collective_id=3, has_side_effects=True
        ),
        name="project",
    )(tokens, segments, w_qkv, up, out_own, gain_one, gain_two)


UNITS = 5
def unit_block(part):
    return lambda u: (jnp.where(u < 3, part * 3 + u, 9 + part * 2 + (u - 3)), 0, 0)


def attend_kernel(
    n, q_ref, k_ref, v_ref, lo_ref, out_part, up_part, down_own, att, lse_ref, of_ref, up, down, out_w,
    qs, ks, ss, obuf, ssem, rsem, lsem, wsend, wrecv, wlocal, zsend, zrecv, fsend, frecv,
):
    u = pl.program_id(0)
    c, t = place()
    d = lax.axis_index("dp")
    shard = down_own.shape[0]
    hidden = down.shape[2]
    peers = [at_peer(c, t, dc, r) for dc, r in PEERS[1:]]

    part = out_part.shape[0] // 2
    mine = pl.ds(pl.multiple_of(c * part, part), part)

    def weight(j, r):
        rows = pl.ds(pl.multiple_of(d * shard, shard), shard)
        src, dst = (
            (down_own.at[:, pl.ds(pl.multiple_of(c * hidden, hidden), hidden)], down.at[t, rows]),
            (up_part, up.at[t]),
            (out_part.at[mine], out_w.at[t, mine]),
        )[j]
        if r == 0:
            return pltpu.make_async_copy(src, dst, wlocal.at[j])
        return pltpu.make_async_remote_copy(
            src, dst, wsend.at[j, r - 1], wrecv.at[j, r - 1], device_id={"tensor": t ^ r}
        )

    def onward(k):
        if k == 2:
            ref, peer = out_w.at[:, mine], {"context": 1 - c}
        else:
            rows = pl.ds(k * part, part)
            ref, peer = up.at[t ^ (1 + k), rows], {"tensor": t ^ (2 - k)}
        return pltpu.make_async_remote_copy(
            ref, ref, fsend.at[k], frecv.at[k], device_id=peer
        )

    def shards(step, up_line):
        src = d - step if up_line else d + step
        rows = pl.ds(pl.multiple_of(jnp.clip(src, 0, n - 1) * shard, shard), shard)
        to = jnp.clip(d + 1 if up_line else d - 1, 0, n - 1)
        k = 0 if up_line else 1
        return pltpu.make_async_remote_copy(
            down.at[:, rows], down.at[:, rows], zsend.at[k, step], zrecv.at[k, step], device_id={"dp": to}
        )

    def line(step, what):
        for up_line in (True, False):
            inside = (d < n - 1) if up_line else (d > 0)
            has = (d >= step) if up_line else (d <= n - 1 - step)
            comes = (d >= step + 1) if up_line else (d <= n - 2 - step)
            if what == "recv":

                @pl.when(comes)
                def _():
                    shards(step, up_line).wait_recv()
            else:

                @pl.when(inside & has)
                def _():
                    if what == "start":
                        shards(step, up_line).start()
                    else:
                        shards(step, up_line).wait_send()
    length = lo_ref.shape[2]
    half = length // 2
    own = half // 4

    @pl.when(u == 0)
    def _():
        greet(peers)
        greet_line(n, d)
        for j in range(3):
            weight(j, 0).start()
        greeted_line(n, d, peers)
        for r in range(1, 4):
            weight(0, r).start()

    qs[...] = q_ref[0] * low(0.125)
    ks[...] = k_ref[0].T
    for start in range(0, length, QB):
        stop = start + QB
        q = qs[:, start:stop]
        lo = lo_ref[0, :, start:stop]
        first = max(0, start - WIN)
        most = jnp.full((8, QB), NEG, full)
        for at in range(first, stop, CHUNK):
            s = nn(ks[at : at + CHUNK, :], q)
            key_pos = at + lax.broadcasted_iota(jnp.int32, (CHUNK, QB), 0)
            allowed = key_pos >= lo
            if at + CHUNK - 1 > start:
                allowed &= key_pos <= start + lax.broadcasted_iota(jnp.int32, (CHUNK, QB), 1)
            s = jnp.where(allowed, s, NEG)
            ss[at - first : at - first + CHUNK, :] = s
            most = jnp.maximum(most, jnp.max(s.reshape(CHUNK // 8, 8, QB), axis=0))
        most = jnp.max(most, axis=0, keepdims=True)
        total = jnp.zeros((8, QB), full)
        acc = jnp.zeros((HD, QB), full)
        for at in range(first, stop, CHUNK):
            p = jnp.exp(ss[at - first : at - first + CHUNK, :] - most)
            total += jnp.sum(p.reshape(CHUNK // 8, 8, QB), axis=0)
            acc += nn(v_ref[0, :, at : at + CHUNK], p.astype(low))
        total = jnp.sum(total, axis=0, keepdims=True)
        lse_ref[0, :, start:stop] = most + jnp.log(total)
        o = acc * (1.0 / total)
        of_ref[0, :, start:stop] = o
        obuf[u, :, start:stop] = o.astype(low)

    @pl.when(u == 0)
    def _():
        weight(0, 0).wait()
        for r in range(1, 4):
            weight(0, r).wait_recv()
        line(0, "start")
        for j, count in ((1, 3), (2, 4)):
            for r in range(1, count):
                weight(j, r).start()

    @pl.when(u == 3)
    def _():
        if n > 2:
            line(0, "recv")
            line(1, "start")
        for k in range(2):
            weight(1, 1 + k).wait_recv()
            onward(k).start()
        weight(2, 0).wait()
        for r in range(1, 4):
            weight(2, r).wait_recv()
        onward(2).start()

    def move(unit, i, source_core):
        dc, r = PEERS[i]
        h, seq = unit_place(unit, source_core)
        dest = pl.multiple_of(((c ^ dc) * 4 + (t ^ r)) * own, own)
        src = obuf.at[unit, :, pl.ds(dest, own)]
        dst = att.at[
            pl.ds(pl.multiple_of((t * 3 + h) * HD, HD), HD), pl.ds(pl.multiple_of(seq * own, own), own)
        ]
        if i == 0:
            return pltpu.make_async_copy(src, dst, lsem.at[unit])
        return pltpu.make_async_remote_copy(
            src, dst, ssem.at[i - 1, unit], rsem.at[i - 1, unit], device_id=at_peer(c, t, dc, r)
        )

    @pl.when(sends(u, c))
    def _():
        for i in range(1, len(PEERS)):
            move(u, i, c).start()
        move(u, 0, c).start()

    @pl.when(u == pl.num_programs(0) - 1)
    def _():
        for step in range(2, n - 1):
            line(step - 1, "recv")
            line(step, "start")
        line(n - 2, "recv")
        for step in range(n - 1):
            line(step, "sent")
        weight(1, 0).wait()
        for j in range(3):
            for r in range(1, 3 if j == 1 else 4):
                weight(j, r).wait_send()
        for k in range(3):
            onward(k).wait()
        for unit in range(UNITS):
            for i, (dc, r) in enumerate(PEERS):

                @pl.when(sends(unit, c))
                def _():
                    if i:
                        move(unit, i, c).wait_send()
                    else:
                        move(unit, i, c).wait()

                if i:

                    @pl.when(sends(unit, c ^ dc))
                    def _():
                        move(unit, i, c ^ dc).wait_recv()


def attend(n, qkv, lo, out_part, up_part, down_own):
    length = lo.shape[2]
    half = length // 2
    own = half // 4
    width, hidden = up_part.shape
    part = lambda p: pl.BlockSpec((1, HD, length), unit_block(p))
    unit = lambda rows, n: pl.BlockSpec((1, rows, n), lambda u: (u, 0, 0))
    heads = 4 * 3 * HD
    return pl.pallas_call(
        functools.partial(attend_kernel, n),
        grid=(UNITS,),
        in_specs=[part(0), part(1), part(2)]
        + [pl.BlockSpec((1, 1, length), lambda u: (u // 3, 0, 0))]
        + [
            pl.BlockSpec(a.shape, lambda u: (0, 0), pipeline_mode=pl.Buffered(1))
            for a in (out_part, up_part, down_own)
        ],
        out_specs=[HBM, unit(1, length), unit(HD, length)] + [HBM] * 3,
        scratch_shapes=[
            pltpu.VMEM((HD, length), low),
            pltpu.VMEM((length, HD), low),
            pltpu.VMEM((WIN + QB, QB), full),
            pltpu.VMEM((UNITS, HD, length), low),
            dma((7, UNITS)),
            dma((7, UNITS)),
            dma((UNITS,)),
            dma((3, 3)),
            dma((3, 3)),
            dma((3,)),
            dma((2, n - 1)),
            dma((2, n - 1)),
            dma((3,)),
            dma((3,)),
        ],
        out_shape=[
            jax.ShapeDtypeStruct((heads, 3 * own), low),
            jax.ShapeDtypeStruct((UNITS, 1, length), full),
            jax.ShapeDtypeStruct((UNITS, HD, length), full),
            shape((4, width, hidden), low),
            shape((4, width, hidden), low),
            shape((4,) + out_part.shape, low),
        ],
        compiler_params=pltpu.CompilerParams(
            vmem_limit_bytes=63 << 20, collective_id=1, has_side_effects=True
        ),
        cost_estimate=pl.CostEstimate(
            flops=UNITS * 18 * 2 * 256 * 1024 * 128, bytes_accessed=20 << 20, transcendentals=0
        ),
        name="attend",
    )(qkv, qkv, qkv, lo, out_part, up_part, down_own)


def add_to(ref, terms):
    for p in range(ref.shape[0]):
        ref[p] = (ref[p].astype(full) + terms(p).astype(full)).astype(low)


def attend_back_kernel(
    n, q_ref, k_ref, v_ref, lo_ref, lse_ref, of_ref, norm_ref, g_ref, gout, gud, side, part_sum,
    dall, gw_sum, zsum, osum, ssum,
    qs, ks, vs, grow, qrow, delta, dqs, soft, dscore, dbuf, gw, gwx, gwr, zr, gud_v, obuf, ogot, sgot, stot, sdp, ssem, rsem, lsem,
    zsend, zrecv, xsend, xrecv, osend, orecv, olocal, vlocal, s_send, s_recv, s_local, dsend, drecv,
):
    u = pl.program_id(0)
    c, t = place()
    d = lax.axis_index("dp")
    shard = gud.shape[1] // n
    length = lo_ref.shape[2]
    own = length // 8
    others = [lax.rem(d + r, n) for r in range(1, n)]
    peers = [at_peer(c, t, dc, r) for dc, r in PEERS[1:]] + [{"dp": o} for o in others]

    def rows_of(j):
        return pl.ds(pl.multiple_of(j * shard, shard), shard)

    def side_tensor(r):
        if r == 0:
            return pltpu.make_async_copy(side.at[t], sgot.at[0], s_local)
        return pltpu.make_async_remote_copy(
            side.at[t ^ r], sgot.at[r], s_send.at[r - 1], s_recv.at[r - 1], device_id={"tensor": t ^ r}
        )

    def side_dp(r):
        return pltpu.make_async_remote_copy(
            stot.at[rows_of(others[r - 1])],
            sdp.at[r - 1],
            dsend.at[r - 1],
            drecv.at[r - 1],
            device_id={"dp": others[r - 1]},
        )

    def line_of(h):
        pair = pl.ds(2 * h, 2)
        return Line(
            n,
            lambda j: gud.at[pair, rows_of(j)],
            lambda k, step: zr.at[h, k, step - 1],
            zsend.at[h],
            zrecv.at[h],
        )

    lines = [line_of(0), line_of(1)]

    def step_of(h, step, arrived=True):
        if arrived and step > 1:
            lines[h].received(step - 1)

        def add(k, j):
            rows = rows_of(j)
            add_to(zr.at[h, k, step - 2], lambda p: gud_v[2 * h + p, rows])

        lines[h].start(step, add)

    def finish(h):
        lines[h].received(n - 1)
        for step in range(2 if h == 0 else 1, n):
            lines[h].sent(step)
        for p in range(2):
            total = gud_v[2 * h + p, rows_of(d)].astype(full)
            up, down = (zr[h, k, n - 2, p].astype(full) for k in range(2))
            total += jnp.where(d > 0, up, 0.0) + jnp.where(d < n - 1, down, 0.0)
            zsum[2 * h + p] = total.astype(low)

    part_rows = gout.shape[2] // 2
    own_half = pl.ds(pl.multiple_of(c * part_rows, part_rows), part_rows)
    other_half = pl.ds(pl.multiple_of((1 - c) * part_rows, part_rows), part_rows)

    def out_grad(r):
        if r == 4:
            return pltpu.make_async_remote_copy(
                gout.at[:, :, other_half], ogot, osend.at[3], orecv.at[3], device_id={"context": 1 - c}
            )
        src, dst = ogot.at[t ^ r], obuf.at[r]
        if r == 0:
            return pltpu.make_async_copy(src, dst, olocal)
        return pltpu.make_async_remote_copy(
            src, dst, osend.at[r - 1], orecv.at[r - 1], device_id={"tensor": t ^ r}
        )

    def other_core():
        return pltpu.make_async_remote_copy(
            gwx.at[1 - c], gwr, xsend, xrecv, device_id={"context": 1 - c}
        )

    def load(i):
        if i == 2:
            return pltpu.make_async_copy(gud, gud_v, vlocal.at[2])
        return pltpu.make_async_copy(part_sum.at[i], zr.at[0, i, 0], vlocal.at[i])

    @pl.when(u == 0)
    def _():
        greet(peers)
        for i in range(3):
            load(i).start()
        gw[...] = jnp.zeros_like(gw)
        greeted(peers)
        out_grad(4).start()
        for r in range(1, 4):
            side_tensor(r).start()
        side_tensor(0).start()
        for i in range(3):
            load(i).wait()
        step_of(0, 2, False)
        step_of(1, 1)

    @pl.when(u == 1)
    def _():
        step_of(0, 3)
        out_grad(4).wait()
        for p in range(4):
            ogot[p] = (ogot[p].astype(full) + gout[p, :, own_half].astype(full)).astype(low)
        for r in range(1, 4):
            out_grad(r).start()
        out_grad(0).start()

    @pl.when(u == 2)
    def _():
        step_of(1, 2)

    @pl.when(u == 3)
    def _():
        side_tensor(0).wait()
        for r in range(1, 4):
            side_tensor(r).wait_recv()
        stot[...] = sum(sgot[r].astype(full) for r in range(4)).astype(low)
        for r in range(1, n):
            side_dp(r).start()

    @pl.when(u == 4)
    def _():
        step_of(1, 3)

    qs[...] = q_ref[0] * low(0.125)
    ks[...] = k_ref[0].T
    vs[...] = v_ref[0].T
    grow[...] = g_ref[0].T
    qrow[...] = qs[...].T
    delta[...] = jnp.sum(g_ref[0].astype(full) * of_ref[0], axis=0, keepdims=True)
    dqs[...] = jnp.zeros_like(dqs)
    for key_start in range(0, length, QB):
        rows = slice(key_start, key_start + QB)
        k, v, key_t = ks[rows, :], vs[rows, :], k_ref[0, :, rows]
        stop = min(key_start + WIN + QB, length)
        key_pos = key_start + lax.broadcasted_iota(jnp.int32, (QB, QB), 0)
        for start in range(key_start, stop, QB):
            cols = slice(start, start + QB)
            held = slice(start - key_start, start - key_start + QB)
            s = nn(k, qs[:, cols]) - lse_ref[0, :, cols]
            allowed = key_pos >= lo_ref[0, :, cols]
            if start == key_start:
                allowed &= key_pos <= start + lax.broadcasted_iota(jnp.int32, (QB, QB), 1)
            p = jnp.exp(jnp.where(allowed, s, NEG))
            dp = nn(v, g_ref[0, :, cols])
            soft[:, held] = p.astype(low)
            dscore[:, held] = (p * (dp - delta[:, cols])).astype(low)
        cols, held = slice(key_start, stop), slice(0, stop - key_start)
        dv = nn(soft[:, held], grow[cols, :])
        dk = nn(dscore[:, held], qrow[cols, :])
        dqs[:, cols] += nn(key_t, dscore[:, held])
        dbuf[u, 1, :, rows] = dk.T.astype(low)
        dbuf[u, 2, :, rows] = dv.T.astype(low)
    dbuf[u, 0] = (dqs[...] * 0.125).astype(low)

    def move(unit, i, source_core):
        dc, r = PEERS[i]
        h, seq = unit_place(unit, source_core)
        dest = pl.multiple_of(((c ^ dc) * 4 + (t ^ r)) * own, own)
        src = dbuf.at[unit, :, :, pl.ds(dest, own)]
        dst = dall.at[t, :, h, :, pl.ds(pl.multiple_of(seq * own, own), own)]
        if i == 0:
            return pltpu.make_async_copy(src, dst, lsem.at[unit])
        return pltpu.make_async_remote_copy(
            src, dst, ssem.at[i - 1, unit], rsem.at[i - 1, unit], device_id=at_peer(c, t, dc, r)
        )

    @pl.when(sends(u, c))
    def _():
        for i in range(1, len(PEERS)):
            move(u, i, c).start()
        move(u, 0, c).start()
        h, _ = unit_place(u, c)
        gw[h] += nn(dbuf[u].reshape(3 * HD, length), norm_ref[0])

    @pl.when(u == pl.num_programs(0) - 1)
    def _():
        wide_rows = [gw[h, p * HD : (p + 1) * HD, :] for p in range(3) for h in range(3)]
        gwx[0] = jnp.concatenate(wide_rows[:6], axis=0).T.astype(low)
        empty = jnp.zeros((3 * HD, gw.shape[2]), full)
        gwx[1] = jnp.concatenate(wide_rows[6:] + [empty], axis=0).T.astype(low)
        other_core().start()
        out_grad(0).wait()
        for r in range(1, 4):
            out_grad(r).wait()
        osum[...] = sum(obuf[r].astype(full) for r in range(4)).T.astype(low)
        other_core().wait()
        gw_sum[...] = (gwx[c].astype(full) + gwr[...].astype(full)).astype(low)
        for step in range(4, n):
            step_of(0, step)
            step_of(1, step)
        finish(0)
        finish(1)
        total = stot[rows_of(d)].astype(full)
        for r in range(1, n):
            side_tensor(r).wait_send() if r < 4 else None
            side_dp(r).wait()
            total += sdp[r - 1].astype(full)
        ssum[...] = total
        for unit in range(UNITS):
            for i, (dc, r) in enumerate(PEERS):

                @pl.when(sends(unit, c))
                def _():
                    if i:
                        move(unit, i, c).wait_send()
                    else:
                        move(unit, i, c).wait()

                if i:

                    @pl.when(sends(unit, c ^ dc))
                    def _():
                        move(unit, i, c ^ dc).wait_recv()


def attend_back(n, qkv, grad_units, lo, lse, attended, normed, grad_out, grad_up_down, side, part_sum):
    length = lo.shape[2]
    own = length // 8
    width = normed.shape[2]
    shard, columns = grad_up_down.shape[1] // n, grad_up_down.shape[2]
    out_rows, local = grad_out.shape[2] // 2, grad_out.shape[1]
    part = lambda p: pl.BlockSpec((1, HD, length), unit_block(p))
    unit = lambda rows, m: pl.BlockSpec((1, rows, m), lambda u: (u, 0, 0))
    once = lambda dims: pl.BlockSpec(dims, lambda u: (0,) * len(dims), pipeline_mode=pl.Buffered(1))
    wide, tall = pltpu.VMEM((HD, length), low), pltpu.VMEM((length, HD), low)
    results = [(width, 2 * 3 * HD), (4, shard, columns), (out_rows, local)]
    return pl.pallas_call(
        functools.partial(attend_back_kernel, n),
        grid=(UNITS,),
        in_specs=[part(0), part(1), part(2)]
        + [
            pl.BlockSpec((1, 1, length), lambda u: (u // 3, 0, 0)),
            unit(1, length),
            unit(HD, length),
            pl.BlockSpec((1, length, width), lambda u: (u // 3, 0, 0)),
            unit(HD, length),
            once(grad_out.shape),
        ]
        + [HBM] * 3,
        out_specs=[HBM] + [once(r) for r in results] + [once((shard, SIDE))],
        scratch_shapes=[
            wide, tall, tall, tall, tall,
            pltpu.VMEM((1, length), full), pltpu.VMEM((HD, length), full),
            pltpu.VMEM((QB, WIN + QB), low), pltpu.VMEM((QB, WIN + QB), low),
            pltpu.VMEM((UNITS, 3, HD, length), low), pltpu.VMEM((3, 3 * HD, width), full),
            pltpu.VMEM((2, width, 6 * HD), low), pltpu.VMEM((width, 6 * HD), low),
            pltpu.VMEM((2, 2, n - 1, 2, shard, columns), low), pltpu.VMEM(grad_up_down.shape, low),
            pltpu.VMEM((4, local, out_rows), low), pltpu.VMEM((4, local, out_rows), low),
            pltpu.VMEM((4, width, SIDE), low), pltpu.VMEM((width, SIDE), low), pltpu.VMEM((n - 1, shard, SIDE), low),
            dma((7, UNITS)), dma((7, UNITS)), dma((UNITS,)),
            dma((2, 2, n - 1)), dma((2, 2, n - 1)), dma, dma, dma((4,)), dma((4,)), dma, dma((3,)),
            dma((3,)), dma((3,)), dma, dma((n - 1,)), dma((n - 1,)),
        ],
        out_shape=[shape((4, 3, 3, HD, 3 * own), low)]
        + [shape(r, low) for r in results]
        + [shape((shard, SIDE), full)],
        compiler_params=pltpu.CompilerParams(
            vmem_limit_bytes=63 << 20, collective_id=2, has_side_effects=True
        ),
        name="attend_back",
    )(qkv, qkv, qkv, lo, lse, attended, normed, grad_units, grad_out, grad_up_down, side, part_sum)


def last_kernel(
    n, dqkv_ref, w_ref, tokens_ref, middle_ref, gains, w_own, up_own, gain_one, gain_two, ssum, gw_sum, zsum, osum,
    grad_in, g_qkv, g_up, g_down, g_out, g_one, g_two,
    rg, rw, ro, down_n, out_t, mine, sums, dqkv, w_all, tokens, middle,
    gsend, grecv, wsend, wrecv, osend, orecv, lsem, csend, crecv, ssend, srecv, clocal, fetch,
):
    c, t = place()
    d = lax.axis_index("dp")
    shard, hidden = rg.shape[1], rg.shape[2]
    cut = n // 2
    group = [at_peer(c, t, dc, r) for dc, r in PEERS[1:]]
    others = [lax.rem(d + r, n) for r in range(1, n)]
    peers = group + [{"dp": o} for o in others]
    greet(peers)
    loads = [
        pltpu.make_async_copy(src, dst, fetch.at[i])
        for i, (src, dst) in enumerate(
            ((tokens_ref, tokens), (w_ref, w_all), (dqkv_ref, dqkv), (middle_ref, middle))
        )
    ]
    for copy in loads:
        copy.start()

    def rows_of(j):
        return pl.ds(pl.multiple_of(j * shard, shard), shard)

    narrow = slice(0, 256)

    def qkv_piece(r, core):
        src, dst = gw_sum.at[rows_of(d if r == 0 else others[r - 1])], rg.at[r]
        if core:
            src, dst = src.at[:, narrow], dst.at[:, narrow]
        if r == 0:
            return pltpu.make_async_copy(src, dst, lsem.at[0])
        return pltpu.make_async_remote_copy(
            src, dst, gsend.at[r - 1], grecv.at[r - 1], device_id={"dp": others[r - 1]}
        )

    def each_core(what):
        for core in range(2):

            @pl.when(c == core)
            def _():
                what(core)

    def up_piece(r):
        src, dst = zsum.at[t ^ r], rw.at[r]
        if r == 0:
            return pltpu.make_async_copy(src, dst, lsem.at[1])
        return pltpu.make_async_remote_copy(
            src, dst, wsend.at[r - 1], wrecv.at[r - 1], device_id={"tensor": t ^ r}
        )

    mine_out = d // cut == c

    def out_piece(r):
        to = d if r == 0 else others[r - 1]
        src, dst = osum.at[rows_of(lax.rem(to, cut))], ro.at[r]
        if r == 0:
            return pltpu.make_async_copy(src, dst, lsem.at[2])
        return pltpu.make_async_remote_copy(
            src, dst, osend.at[r - 1], orecv.at[r - 1], device_id={"dp": to}
        )

    def start_all(core):
        for r in range(1, n):
            qkv_piece(r, core).start()
        qkv_piece(0, core).start()

    greeted(peers)
    each_core(start_all)
    for r in range(1, 4):
        up_piece(r).start()
    up_piece(0).start()
    for r in range(1, n):

        @pl.when(others[r - 1] // cut == c)
        def _():
            out_piece(r).start()

    @pl.when(mine_out)
    def _():
        out_piece(0).start()

    for copy in loads:
        copy.wait()
    @pl.loop(0, tokens.shape[0] // QB)
    def _(m):
        rows = pl.ds(pl.multiple_of(m * QB, QB), QB)
        r = tn(dqkv[:, rows], w_all[...])
        v = tokens[rows, :].astype(full)
        inv = lax.rsqrt(jnp.mean(v * v, axis=-1, keepdims=True) + epsilon)
        rg_ = r * gains[0:1, :]
        grad = inv * (rg_ - v * (inv * inv * jnp.mean(rg_ * v, axis=-1, keepdims=True)))
        grad_in[rows, :] = (middle[rows, :] + grad).astype(low)

    def halves(j):
        half = pl.ds(pl.multiple_of(c * hidden, hidden), hidden)
        src, dst = (
            (mine.at[0], g_qkv.at[:, half]),
            (mine.at[1], g_up.at[:, half]),
            (down_n, g_down.at[:, half]),
            (out_t, g_out),
        )[j]
        return (
            pltpu.make_async_copy(src, dst, clocal.at[j]),
            pltpu.make_async_remote_copy(
                src, dst, csend.at[j], crecv.at[j], device_id={"context": 1 - c}
            ),
        )

    def deliver(j):
        for copy in halves(j):
            copy.start()

    up_piece(0).wait()
    for r in range(1, 4):
        up_piece(r).wait_recv()
    main = hidden - SIDE
    mine[1, :, :main] = sum(rw[r, :, :main].astype(full) for r in range(4))
    mine[1, :, main:] = ssum[...]
    down_n[...] = sum(rw[r, :, main:].astype(full) for r in range(4))
    deliver(1)
    deliver(2)

    @pl.when(mine_out)
    def _():
        out_piece(0).wait()
        for r in range(1, n):
            out_piece(r).wait_recv()
        out_t[...] = sum(ro[r].astype(full) for r in range(n)).T
        deliver(3)

    def take(core):
        qkv_piece(0, core).wait()
        for r in range(1, n):
            qkv_piece(r, core).wait_recv()
        if core:
            mine[0, :, narrow] = sum(rg[r, :, narrow].astype(full) for r in range(n))
            mine[0, :, 256:] = jnp.zeros((shard, hidden - 256), full)
        else:
            mine[0] = sum(rg[r].astype(full) for r in range(n))

    each_core(take)
    deliver(0)
    lane = lax.broadcasted_iota(jnp.int32, (shard, 128), 1)
    halves_of = [jnp.concatenate([w_own[0], w_own[1]], axis=1), jnp.pad(w_own[2], ((0, 0), (0, osum.shape[1])))]
    w_mine = jnp.where(c == 0, halves_of[0].astype(full), halves_of[1].astype(full))
    up_mine = up_own[:, pl.ds(pl.multiple_of(c * hidden, hidden), hidden)].astype(full)
    first = jnp.sum(w_mine * mine[0], axis=1, keepdims=True)
    second = jnp.sum(up_mine * mine[1], axis=1, keepdims=True)
    sums[0] = jnp.where(lane == 0, first, jnp.where(lane == 1, second, 0.0)).T[:8]

    def gain_piece(i):
        dc, r = PEERS[i]
        return pltpu.make_async_remote_copy(
            sums.at[0], sums.at[i], ssend.at[i - 1], srecv.at[i - 1], device_id=at_peer(c, t, dc, r)
        )

    for i in range(1, len(PEERS)):
        gain_piece(i).start()
    for i in range(1, len(PEERS)):
        gain_piece(i).wait()
    total = sum(sums[i] for i in range(len(PEERS)))
    g_one[...] = total[0:1, :] / gain_one[...].astype(full)
    g_two[...] = total[1:2, :] / gain_two[...].astype(full)

    for j in range(3):
        for copy in halves(j):
            copy.wait()

    @pl.when(mine_out)
    def _():
        local, away = halves(3)
        local.wait()
        away.wait_send()

    @pl.when(jnp.logical_not(mine_out))
    def _():
        halves(3)[1].wait_recv()

    for r in range(1, 4):
        up_piece(r).wait_send()

    def sent(core):
        for r in range(1, n):
            qkv_piece(r, core).wait_send()

    each_core(sent)
    for r in range(1, n):

        @pl.when(others[r - 1] // cut == c)
        def _():
            out_piece(r).wait_send()


def last(n, dqkv, w_all, tokens, middle, gains, w_own, up_own, gain_one, gain_two, ssum, gw_sum, zsum, osum):
    rows, width = tokens.shape
    shard, hidden = zsum.shape[1], gw_sum.shape[1]
    local = osum.shape[1]
    return pl.pallas_call(
        functools.partial(last_kernel, n),
        in_specs=[HBM] * 4 + [VMEM] * 6 + [ANY] * 3,
        out_specs=[VMEM] + [ANY] * 4 + [VMEM] * 2,
        out_shape=[
            shape((rows, width), low),
            shape((shard, 2 * hidden), full),
            shape((shard, 2 * hidden), full),
            shape((shard, 2 * hidden), full),
            shape((local, shard), full),
            shape((1, shard), full),
            shape((1, shard), full),
        ],
        scratch_shapes=[
            pltpu.VMEM((n, shard, hidden), low),
            pltpu.VMEM((4, shard, 2 * hidden - SIDE), low),
            pltpu.VMEM((n, shard, local), low),
            pltpu.VMEM((shard, hidden), full),
            pltpu.VMEM((local, shard), full),
            pltpu.VMEM((2, shard, hidden), full),
            pltpu.VMEM((8, 8, shard), full),
            pltpu.VMEM(dqkv.shape, low), pltpu.VMEM(w_all.shape, low),
            pltpu.VMEM((rows, width), low), pltpu.VMEM((rows, width), full),
            dma((n - 1,)), dma((n - 1,)), dma((3,)), dma((3,)), dma((n - 1,)), dma((n - 1,)), dma((3,)),
            dma((4,)), dma((4,)), dma((7,)), dma((7,)), dma((4,)), dma((4,)),
        ],
        compiler_params=pltpu.CompilerParams(
            vmem_limit_bytes=63 << 20, collective_id=4, has_side_effects=True
        ),
        name="last",
    )(dqkv, w_all, tokens, middle, gains, w_own, up_own, gain_one, gain_two, ssum, gw_sum, zsum, osum)


def close_kernel(*refs):
    count = len(refs) // 2
    for i, (src, dst) in enumerate(zip(refs[:count], refs[count:])):
        if i == 2:
            local = dst.shape[2]
            for p in range(3):
                dst[p] = src[:, p * local : (p + 1) * local]
        else:
            dst[...] = src[...]


def close(result, grad_input, own_attn, *others):
    arrays = (result, grad_input, own_attn, *others)
    rows = lambda a: pl.BlockSpec((a.shape[0] // 2, a.shape[1]), lambda i: (i, 0))
    shard, local = own_attn.shape[0], others[0].shape[0]
    parts = pl.BlockSpec((3, shard // 2, local), lambda i: (0, i, 0))
    outs = [shape(a.shape, a.dtype) for a in arrays]
    outs[2] = shape((3, shard, local), full)
    return pl.pallas_call(
        close_kernel,
        grid=(2,),
        in_specs=[rows(a) for a in arrays],
        out_specs=[parts if i == 2 else rows(a) for i, a in enumerate(arrays)],
        out_shape=outs,
        compiler_params=pltpu.CompilerParams(vmem_limit_bytes=63 << 20),
        name="close",
    )(*arrays)


def gelu_and_slope(v):
    k0 = math.sqrt(2.0 / math.pi)
    square = v * v
    th = jnp.tanh(v * (k0 + (k0 * 0.044715) * square))
    half = 0.5 + 0.5 * th
    slope = half + (v * half) * ((1.0 - th) * (k0 + (3.0 * 0.044715 * k0) * square))
    return v * half, slope


def feed_kernel(
    dp, att, proj, tokens, cot, gains, w_t, up_ref, down_ref,
    result, middle, gout, gud, side, part_sum, units, w_all,
    x, g, x_t, g_t, up, down, act, gh, out, back, proj_w, sent, got, gbuf, sbuf, gatt,
    xsend, xrecv, wsend, wrecv, wlocal, zsend, zrecv, glocal, usend, urecv, ulocal, load,
):
    c, t = place()
    d = lax.axis_index("dp")
    rows, width = tokens.shape
    own = rows // 3
    shard = width // dp
    n = up_ref.shape[2]
    local = proj.shape[2]
    other = {"context": 1 - c}
    peers = [at_peer(c, t, dc, r) for dc, r in PEERS[1:]]
    mine, theirs = slice(0, rows), slice(rows, 2 * rows)
    block = rows // 3

    def cross(k):
        src, dst = (
            (cot, g.at[theirs]),
            (x.at[mine], x.at[theirs]),
            (sent.at[0], got.at[0]),
            (sent.at[1], got.at[1]),
        )[k]
        return pltpu.make_async_remote_copy(src, dst, xsend.at[k], xrecv.at[k], device_id=other)

    half = pl.ds(pl.multiple_of(c * (w_t.shape[0] // 2), 8), w_t.shape[0] // 2)

    def over_tensor(r):
        if r == 4:
            ref = w_all.at[:, half]
            return pltpu.make_async_remote_copy(ref, ref, wsend.at[3], wrecv.at[3], device_id=other)
        src, dst = w_t.at[half], w_all.at[t, half]
        if r == 0:
            return pltpu.make_async_copy(src, dst, wlocal)
        return pltpu.make_async_remote_copy(
            src, dst, wsend.at[r - 1], wrecv.at[r - 1], device_id={"tensor": t ^ r}
        )

    def rows_of(i):
        return pl.ds(pl.multiple_of(i * shard, shard), shard)

    line = Line(
        dp,
        lambda i: gbuf.at[0, :, rows_of(i)],
        lambda k, step: part_sum.at[k],
        zsend,
        zrecv,
    )

    def keep(j):
        if j == 2:
            return pltpu.make_async_copy(sbuf, side, glocal.at[2])
        return pltpu.make_async_copy(gbuf.at[j], gud.at[pl.ds(2 * j, 2)], glocal.at[j])

    def leave(whole, i):
        dc, r = PEERS[i]
        to_c, to_t = c ^ dc, t ^ r
        head = to_t * 3 + (0 if whole else to_c)
        count, first = (3, 0) if whole else (2, 3)
        seq = 2 * to_c if whole else 1
        src = gatt.at[pl.ds(head, count), :, pl.ds(pl.multiple_of(seq * own, own), own)]
        dst = units.at[pl.ds(first, count), :, pl.ds(pl.multiple_of((c * 4 + t) * own, own), own)]
        k = 0 if whole else 1
        if i == 0:
            return pltpu.make_async_copy(src, dst, ulocal.at[k])
        return pltpu.make_async_remote_copy(
            src, dst, usend.at[k, i - 1], urecv.at[k, i - 1], device_id=at_peer(c, t, dc, r)
        )

    loads = [
        pltpu.make_async_copy(ref.at[p], dst.at[p // 2, :, pl.ds((p % 2) * n, n)], load.at[i, p])
        for i, (ref, dst) in enumerate(((up_ref, up), (down_ref, down)))
        for p in range(4)
    ]
    greet(peers)
    greet_line(dp, d)
    for copy in loads:
        copy.start()
    for p in range(4):
        proj_w[:, p * local : (p + 1) * local] = proj[p]
    greeted_line(dp, d, peers)
    cross(0).start()
    for r in range(1, 4):
        over_tensor(r).start()
    over_tensor(0).start()
    for m in range(0, rows, block):
        part = slice(m, m + block)
        v = tokens[part, :].astype(full) + nn(proj_w[...], att[:, part]).T
        middle[part, :] = v
        inv = lax.rsqrt(jnp.mean(v * v, axis=-1, keepdims=True) + epsilon)
        x[part, :] = (v * inv * gains[1:2, :]).astype(low)
    cross(1).start()
    g[mine, :] = cot[...]
    g_t[:, mine] = cot[...].T
    x_t[:, mine] = x[mine, :].T
    for copy in loads:
        copy.wait()

    def hidden(side):
        @pl.loop(0, 6)
        def _(i):
            j = i // 3
            part = pl.ds(pl.multiple_of((side * 3 + i % 3) * block, block), block)
            pre = nn(x[part, :], up[j])
            ga = nn(g[part, :], down[j])
            a, slope = gelu_and_slope(pre)
            act[j, part, :] = a.astype(low)
            gh[j, part, :] = (ga * slope).astype(low)

    def branch(left, right, part):
        return nt(left[0, part, :], right[0]) + nt(left[1, part, :], right[1])

    hidden(0)
    cross(0).wait_recv()
    cross(1).wait_recv()
    hidden(1)

    def cut(side, left, right, put):
        @pl.loop(0, 3)
        def _(i):
            here = pl.ds(pl.multiple_of(i * block, block), block)
            part = pl.ds(pl.multiple_of(side * rows + i * block, block), block)
            put(here, branch(left, right, part))

    def put_sent(k):
        def put(here, value):
            sent[k, here, :] = value.astype(low)

        return put

    def put_own(ref):
        def put(here, value):
            ref[here, :] = value

        return put

    cut(1, gh, up, put_sent(0))
    cross(2).start()
    cut(0, gh, up, put_own(back))
    over_tensor(0).wait()
    for r in range(1, 4):
        over_tensor(r).wait_recv()
    over_tensor(4).start()
    x_t[:, theirs] = x[theirs, :].T
    g_t[:, theirs] = g[theirs, :].T
    cross(1).wait_send()
    cross(2).wait_recv()
    gain = gains[1:2, :]
    low_t = x
    for m in range(0, rows, block):
        part = slice(m, m + block)
        r = (back[part, :] + got[0, part, :].astype(full)) * gain
        v = middle[part, :]
        inv = lax.rsqrt(jnp.mean(v * v, axis=-1, keepdims=True) + epsilon)
        grad = inv * (r - v * (inv * inv * jnp.mean(r * v, axis=-1, keepdims=True)))
        back[part, :] = cot[part, :].astype(full) + grad
        x[part, :] = back[part, :].astype(low)
        low_t[rows : rows + width, part] = x[part, :].T
        grad = tn(proj_w[...], low_t[rows : rows + width, part]).astype(low)
        gatt[:, :, part] = grad.reshape(gatt.shape[0], HD, block)
    for whole in (True, False):
        for i in range(1, len(PEERS)):
            leave(whole, i).start()
        leave(whole, 0).start()

    def weight_grad(j, a, left_t, right):
        @pl.loop(0, 3)
        def _(i):
            part = pl.ds(pl.multiple_of(i * (width // 3), width // 3), width // 3)
            grad = nn(left_t[part, :], right[j]).astype(low)
            main = n - SIDE
            for p in range(2):
                if a:
                    gbuf[j, p, part, main:] = grad[:, p * n : (p + 1) * n]
                else:
                    gbuf[j, p, part, :main] = grad[:, p * n : p * n + main]
                    sbuf[2 * j + p, part, :] = grad[:, p * n + main : (p + 1) * n]

    weight_grad(0, 0, x_t, gh)
    weight_grad(0, 1, g_t, act)
    line.start(1, None)
    keep(0).start()
    cut(1, act, down, put_sent(1))
    cross(3).start()
    weight_grad(1, 0, x_t, gh)
    weight_grad(1, 1, g_t, act)
    keep(1).start()
    keep(2).start()
    cut(0, act, down, put_own(out))
    for p in range(4):
        gout[p] = nn(att[p * local : (p + 1) * local, :], x[mine, :]).astype(low)
    cross(3).wait_recv()
    result[...] = (middle[...] + out[...] + got[1].astype(full)).astype(low)
    middle[...] = back[...]
    for k in (0, 2, 3):
        cross(k).wait_send()
    for r in range(1, 4):
        over_tensor(r).wait_send()
    over_tensor(4).wait()
    line.received(1)
    line.sent(1)
    for j in range(3):
        keep(j).wait()
    for whole in (True, False):
        for i in range(len(PEERS)):
            leave(whole, i).wait()


def feed(dp, att, proj, tokens, cot, gains, w_t, up, down):
    rows, width = tokens.shape
    pieces, _, n = up.shape
    own = rows // 3
    assert pieces == 4 and dp > 2 and rows == width
    return pl.pallas_call(
        functools.partial(feed_kernel, dp),
        in_specs=[VMEM] * 6 + [HBM] * 2,
        out_specs=[VMEM] * 3 + [HBM] * 5,
        out_shape=[
            shape((rows, width), low),
            shape((rows, width), full),
            shape((4, proj.shape[2], width), low),
            shape((4, width, 2 * n - SIDE), low),
            shape((4, width, SIDE), low),
            shape((2, 2, width // dp, 2 * n - SIDE), low),
            shape((UNITS, HD, 8 * own), low),
            shape((4,) + w_t.shape, low),
        ],
        scratch_shapes=[pltpu.VMEM((2 * rows, width), low)] * 2
        + [pltpu.VMEM((width, 2 * rows), low)] * 2
        + [pltpu.VMEM((2, width, 2 * n), low)] * 2
        + [pltpu.VMEM((2, 2 * rows, 2 * n), low)] * 2
        + [pltpu.VMEM((rows, width), full)] * 2
        + [pltpu.VMEM((width, width), low)]
        + [pltpu.VMEM((2, rows, width), low)] * 2
        + [pltpu.VMEM((2, 2, width, 2 * n - SIDE), low), pltpu.VMEM((4, width, SIDE), low)]
        + [pltpu.VMEM((12, HD, rows), low)]
        + [dma((4,)), dma((4,)), dma((4,)), dma((4,)), dma]
        + [dma((2, 1)), dma((2, 1)), dma((3,)), dma((2, 7)), dma((2, 7)), dma((2,)), dma((2, 4))],
        compiler_params=pltpu.CompilerParams(
            vmem_limit_bytes=63 << 20, collective_id=5, has_side_effects=True
        ),
        name="feed",
    )(att, proj, tokens, cot, gains, w_t, up, down)


def per_device(tokens, segments, w_qkv, w_out, w_in, w_back, gain_attn, gain_mlp, cotangent):
    sequences, own, width = tokens.shape
    assert lax.axis_size("tensor") == 4 and lax.axis_size("context") == 2 and sequences == 3
    n = lax.axis_size("dp")
    length = segments.shape[1]
    shard = w_qkv.shape[0]
    local = w_qkv.shape[2]
    rows = sequences * own
    parts = w_qkv.transpose(1, 0, 2)
    gain_one, gain_two = gain_attn.reshape(1, shard), gain_mlp.reshape(1, shard)
    qkv, normed_units, w_t, up_part, out_part, gains, lo = project(
        n, tokens, segments, parts, w_in, w_out, gain_one, gain_two
    )
    attended, log_totals, out_full, w_up, w_down, w_proj = attend(
        n, qkv, lo, out_part, up_part, w_back.T
    )
    flat = tokens.reshape(rows, width)
    result, grad_middle, grad_out, grad_up_down, side, part_sum, grad_units, w_all = feed(
        n, attended, w_proj, flat, cotangent.reshape(rows, width), gains, w_t, w_up, w_down
    )
    grad_projected, gw_sum, zsum, osum, ssum = attend_back(
        n, qkv, grad_units, lo, log_totals, out_full, normed_units, grad_out, grad_up_down, side, part_sum
    )
    grad_input, own_attn, own_up, own_down, own_proj, own_one, own_two = last(
        n,
        grad_projected.reshape(12 * local, rows),
        w_all.reshape(12 * local, width),
        flat,
        grad_middle,
        gains,
        parts,
        w_in,
        gain_one,
        gain_two,
        ssum,
        gw_sum,
        zsum,
        osum,
    )
    result, grad_input, own_attn, own_proj, own_up, own_down = close(
        result, grad_input, own_attn, own_proj, own_up, own_down
    )
    return (
        result.reshape(sequences, own, width),
        grad_input.reshape(sequences, own, width),
        own_attn.transpose(1, 0, 2),
        own_proj,
        own_up,
        own_down.T,
        own_one.reshape(shard),
        own_two.reshape(shard),
    )


def solution(mesh):
    return jax.shard_map(
        per_device,
        mesh=mesh,
        in_specs=(
            P("dp", ("context", "tensor"), None),
            P("dp", None),
            P("dp", None, "tensor"),
            P("tensor", "dp"),
            P("dp", "tensor"),
            P("tensor", "dp"),
            P("dp"),
            P("dp"),
            P("dp", ("context", "tensor"), None),
        ),
        out_specs=(
            P("dp", ("context", "tensor"), None),
            P("dp", ("context", "tensor"), None),
            P("dp", None, "tensor"),
            P("tensor", "dp"),
            P("dp", "tensor"),
            P("tensor", "dp"),
            P("dp"),
            P("dp"),
        ),
        check_vma=False,
    )
```

profile of v0, /device:TPU:1, one launch (start us, length us, event | category | flops | bytes accessed | tf_op | source)
XLA Modules:
  0.0 254.9 jit_solution(9088981521538317381)
XLA Ops:
  0.6 1.2 reshape.46.gain_one
  1.9 1.2 reshape.47.gain_two
  3.1 51.5 %project.1 = (bf16[15,64,2048]{2,1,0:T(8,128)(2,1)}, bf16[2,2048,768]{2,1,0:T(8,128)(2,1)}, bf16[576,768]{1,0:T(8,128)(2,1)}, bf16[768,384]{1,0:T(8,128)(2,1)}, ...) custom-call(bf16[3,256,768]{2,1,0:T(8,128)(2,1)} %tokens.1, s32[3,2048]{1,0:T(4,128)} %segments.1, ...), custom_call_target="tpu_custom_call" | custom-call | tf_op jit(solution)/shard_map/project/pallas_call | solution.py:328
  54.6 55.4 %attend.1 = (bf16[768,768]{1,0:T(8,128)(2,1)}, f32[5,1,2048]{2,1,0:T(1,128)}, f32[5,64,2048]{2,1,0:T(8,128)}, bf16[4,768,384]{2,1,0:T(8,128)(2,1)}, bf16[4,768,3...) custom-call(bf16[15,64,2048]{2,1,0:T(8,128)(2,1)} %get-tuple-element.47.q_ref.k_ref.v_ref, ...), custom_call_target="tpu_custom_call" | custom-call | flops 6039797760 | bytes 20971520 | tf_op jit(solution)/shard_map/attend/pallas_call | solution.py:555
  110.1 47.1 %feed.1 = (bf16[768,768]{1,0:T(8,128)(2,1)}, f32[768,768]{1,0:T(8,128)}, bf16[4,192,768]{2,1,0:T(8,128)(2,1)}, bf16[4,768,640]{2,1,0:T(8,128)(2,1)}, bf16[4,768,...) custom-call(bf16[768,768]{1,0:T(8,128)(2,1)} %get-tuple-element.51.a, ...), custom_call_target="tpu_custom_call" | custom-call | tf_op jit(solution)/shard_map/feed/pallas_call | solution.py:1365
  157.1 64.2 %attend_back.1 = (bf16[4,3,3,64,768]{4,3,2,1,0:T(8,128)(2,1)}, bf16[768,384]{1,0:T(8,128)(2,1)}, bf16[4,192,640]{2,1,0:T(8,128)(2,1)}, bf16[384,192]{1,0:T(8,128)(2,1)}, f32[192,128]{1,0:T(8,128)}) custom-call(bf16[15,64,2048]{2,1,0:T(8,128)(2,1)} %get-tuple-element.47.q_ref.k_ref.v_ref, bf16[15,64,2048]{2,1,0:T(8,128)(2,1)} %get-tuple-element.47.q_ref.k_ref.v_ref, ...), custom_call_target="tpu_custom_call" | custom-call | tf_op jit(solution)/shard_map/attend_back/pallas_call | solution.py:842
  221.3 28.7 %last.1 = (bf16[768,768]{1,0:T(8,128)(2,1)}, f32[192,768]{1,0:T(8,128)}, f32[192,768]{1,0:T(8,128)}, f32[192,768]{1,0:T(8,128)}, f32[192,192]{1,0:T(8,128)}, /*index=5*/f32[1,192]{1,0:T(1,128)}, f32[1,192]{1,0:T(1,128)}) custom-call(bf16[2304,768]{1,0:T(8,128)(2,1)} %bitcast.15, bf16[2304,768]{1,0:T(8,128)(2,1)} %bitcast.14, bf16[768,768]{1,0:T(8,128)(2,1)} %bitcast.13, ...), custom_call_target="tpu_custom_call" | custom-call | tf_op jit(solution)/shard_map/last/pallas_call | solution.py:1079
  250.0 0.0 copy-start.1
  250.0 0.0 copy-start
  250.0 3.7 %close.1 = (bf16[768,768]{1,0:T(8,128)(2,1)}, bf16[768,768]{1,0:T(8,128)(2,1)}, f32[3,192,192]{2,1,0:T(8,128)}, f32[192,192]{1,0:T(8,128)}, f32[192,768]{1,0:T(8,128)}, /*index=5*/f32[192,768]{1,0:T(8,128)}) custom-call(bf16[768,768]{1,0:T(8,128)(2,1)} %get-tuple-element.57.refs_0_, bf16[768,768]{1,0:T(8,128)(2,1)} %get-tuple-element.73.refs_1_, ...), custom_call_target="tpu_custom_call" | custom-call | tf_op jit(solution)/shard_map/close/pallas_call | solution.py:1130
  253.7 0.0 copy-done.1
  253.7 0.6 copy.19
  254.3 0.0 copy-done
  254.3 0.6 copy.20
Async XLA Ops:
  250.0 3.7 %copy-start.1 = (f32[1,192]{1,0:T(1,128)S(1)}, f32[1,192]{1,0:T(1,128)}, u32[]{:S(2)}) copy-start(f32[1,192]{1,0:T(1,128)} %get-tuple-element.84) | copy-start | bytes 2308
  250.0 4.3 %copy-start = (f32[1,192]{1,0:T(1,128)S(1)}, f32[1,192]{1,0:T(1,128)}, u32[]{:S(2)}) copy-start(f32[1,192]{1,0:T(1,128)} %get-tuple-element.85) | copy-start | bytes 2308
where the time goes:
time: 256 us; the launch traced here: 255 us
  Pallas kernels  251 us (98%)
  local copies, waits for them, and re-layouts  3.58 us (1%)
    pallas_call x1, Pallas kernels, attend_back(): pl.pallas_call(functools.partial(attend_back_kernel, n), grid=(UNITS,), i...  64.2 us
    pallas_call x1, Pallas kernels, attend(): pl.pallas_call(functools.partial(attend_kernel, n), grid=(UNITS,), in_spe...  55.4 us
    pallas_call x1, Pallas kernels, project(): pl.pallas_call(functools.partial(project_kernel, n), in_specs=[HBM, VMEM,...  51.5 us
    pallas_call x1, Pallas kernels, feed(): pl.pallas_call(functools.partial(feed_kernel, dp), in_specs=[VMEM] * 6 +...  47.1 us
    pallas_call x1, Pallas kernels, last(): pl.pallas_call(functools.partial(last_kernel, n), in_specs=[HBM] * 4 + [V...  28.7 us

commit v1 on v0

--- a/solution.py
+++ b/solution.py
@@ -439,6 +439,8 @@
         greeted_line(n, d, peers)
         for r in range(1, 4):
             weight(0, r).start()
+        for r in range(1, 3):
+            weight(1, r).start()
 
     qs[...] = q_ref[0] * low(0.125)
     ks[...] = k_ref[0].T
@@ -476,9 +478,8 @@
         for r in range(1, 4):
             weight(0, r).wait_recv()
         line(0, "start")
-        for j, count in ((1, 3), (2, 4)):
-            for r in range(1, count):
-                weight(j, r).start()
+        for r in range(1, 4):
+            weight(2, r).start()
 
     @pl.when(u == 3)
     def _():
@@ -704,26 +705,22 @@
         for r in range(1, 4):
             side_tensor(r).start()
         side_tensor(0).start()
+        step_of(1, 1)
         for i in range(3):
             load(i).wait()
         step_of(0, 2, False)
-        step_of(1, 1)
 
     @pl.when(u == 1)
     def _():
-        step_of(0, 3)
         out_grad(4).wait()
         for p in range(4):
             ogot[p] = (ogot[p].astype(full) + gout[p, :, own_half].astype(full)).astype(low)
         for r in range(1, 4):
             out_grad(r).start()
         out_grad(0).start()
+        step_of(1, 2)
 
     @pl.when(u == 2)
-    def _():
-        step_of(1, 2)
-
-    @pl.when(u == 3)
     def _():
         side_tensor(0).wait()
         for r in range(1, 4):
@@ -731,6 +728,10 @@
         stot[...] = sum(sgot[r].astype(full) for r in range(4)).astype(low)
         for r in range(1, n):
             side_dp(r).start()
+
+    @pl.when(u == 3)
+    def _():
+        step_of(0, 3)
 
     @pl.when(u == 4)
     def _():

time: 256 us -> 251 us (0.980)
  Pallas kernels: 251 us -> 246 us
where the time goes in v1:
time: 251 us; the launch traced here: 250 us
  Pallas kernels  246 us (98%)
  local copies, waits for them, and re-layouts  3.58 us (1%)
    pallas_call x1, Pallas kernels, attend_back(): pl.pallas_call(functools.partial(attend_back_kernel, n), grid=(UNITS,), i...  62.7 us
    pallas_call x1, Pallas kernels, attend(): pl.pallas_call(functools.partial(attend_kernel, n), grid=(UNITS,), in_spe...  53.4 us
    pallas_call x1, Pallas kernels, project(): pl.pallas_call(functools.partial(project_kernel, n), in_specs=[HBM, VMEM,...  51.5 us
    pallas_call x1, Pallas kernels, feed(): pl.pallas_call(functools.partial(feed_kernel, dp), in_specs=[VMEM] * 6 +...  48.2 us
    pallas_call x1, Pallas kernels, last(): pl.pallas_call(functools.partial(last_kernel, n), in_specs=[HBM] * 4 + [V...  26.3 us

profile of v1, /device:TPU:1, one launch (start us, length us, event | category | flops | bytes accessed | tf_op | source)
XLA Modules:
  0.0 250.2 jit_solution(4707330980933086800)
XLA Ops:
  0.6 1.2 reshape.46.gain_one
  1.9 1.2 reshape.47.gain_two
  3.1 51.5 %project.1 = (bf16[15,64,2048]{2,1,0:T(8,128)(2,1)}, bf16[2,2048,768]{2,1,0:T(8,128)(2,1)}, bf16[576,768]{1,0:T(8,128)(2,1)}, bf16[768,384]{1,0:T(8,128)(2,1)}, ...) custom-call(bf16[3,256,768]{2,1,0:T(8,128)(2,1)} %tokens.1, s32[3,2048]{1,0:T(4,128)} %segments.1, ...), custom_call_target="tpu_custom_call" | custom-call | tf_op jit(solution)/shard_map/project/pallas_call | solution.py:328
  54.6 53.4 %attend.1 = (bf16[768,768]{1,0:T(8,128)(2,1)}, f32[5,1,2048]{2,1,0:T(1,128)}, f32[5,64,2048]{2,1,0:T(8,128)}, bf16[4,768,384]{2,1,0:T(8,128)(2,1)}, bf16[4,768,3...) custom-call(bf16[15,64,2048]{2,1,0:T(8,128)(2,1)} %get-tuple-element.47.q_ref.k_ref.v_ref, ...), custom_call_target="tpu_custom_call" | custom-call | flops 6039797760 | bytes 20971520 | tf_op jit(solution)/shard_map/attend/pallas_call | solution.py:556
  108.1 48.2 %feed.1 = (bf16[768,768]{1,0:T(8,128)(2,1)}, f32[768,768]{1,0:T(8,128)}, bf16[4,192,768]{2,1,0:T(8,128)(2,1)}, bf16[4,768,640]{2,1,0:T(8,128)(2,1)}, bf16[4,768,...) custom-call(bf16[768,768]{1,0:T(8,128)(2,1)} %get-tuple-element.51.a, ...), custom_call_target="tpu_custom_call" | custom-call | tf_op jit(solution)/shard_map/feed/pallas_call | solution.py:1366
  156.3 62.7 %attend_back.1 = (bf16[4,3,3,64,768]{4,3,2,1,0:T(8,128)(2,1)}, bf16[768,384]{1,0:T(8,128)(2,1)}, bf16[4,192,640]{2,1,0:T(8,128)(2,1)}, bf16[384,192]{1,0:T(8,128)(2,1)}, f32[192,128]{1,0:T(8,128)}) custom-call(bf16[15,64,2048]{2,1,0:T(8,128)(2,1)} %get-tuple-element.47.q_ref.k_ref.v_ref, bf16[15,64,2048]{2,1,0:T(8,128)(2,1)} %get-tuple-element.47.q_ref.k_ref.v_ref, ...), custom_call_target="tpu_custom_call" | custom-call | tf_op jit(solution)/shard_map/attend_back/pallas_call | solution.py:843
  219.0 26.3 %last.1 = (bf16[768,768]{1,0:T(8,128)(2,1)}, f32[192,768]{1,0:T(8,128)}, f32[192,768]{1,0:T(8,128)}, f32[192,768]{1,0:T(8,128)}, f32[192,192]{1,0:T(8,128)}, /*index=5*/f32[1,192]{1,0:T(1,128)}, f32[1,192]{1,0:T(1,128)}) custom-call(bf16[2304,768]{1,0:T(8,128)(2,1)} %bitcast.15, bf16[2304,768]{1,0:T(8,128)(2,1)} %bitcast.14, bf16[768,768]{1,0:T(8,128)(2,1)} %bitcast.13, ...), custom_call_target="tpu_custom_call" | custom-call | tf_op jit(solution)/shard_map/last/pallas_call | solution.py:1080
  245.3 0.0 copy-start.1
  245.3 0.0 copy-start
  245.3 3.7 %close.1 = (bf16[768,768]{1,0:T(8,128)(2,1)}, bf16[768,768]{1,0:T(8,128)(2,1)}, f32[3,192,192]{2,1,0:T(8,128)}, f32[192,192]{1,0:T(8,128)}, f32[192,768]{1,0:T(8,128)}, /*index=5*/f32[192,768]{1,0:T(8,128)}) custom-call(bf16[768,768]{1,0:T(8,128)(2,1)} %get-tuple-element.57.refs_0_, bf16[768,768]{1,0:T(8,128)(2,1)} %get-tuple-element.73.refs_1_, ...), custom_call_target="tpu_custom_call" | custom-call | tf_op jit(solution)/shard_map/close/pallas_call | solution.py:1131
  249.0 0.0 copy-done.1
  249.0 0.6 copy.19
  249.6 0.0 copy-done
  249.6 0.6 copy.20
Async XLA Ops:
  245.3 3.7 %copy-start.1 = (f32[1,192]{1,0:T(1,128)S(1)}, f32[1,192]{1,0:T(1,128)}, u32[]{:S(2)}) copy-start(f32[1,192]{1,0:T(1,128)} %get-tuple-element.84) | copy-start | bytes 2308
  245.3 4.3 %copy-start = (f32[1,192]{1,0:T(1,128)S(1)}, f32[1,192]{1,0:T(1,128)}, u32[]{:S(2)}) copy-start(f32[1,192]{1,0:T(1,128)} %get-tuple-element.85) | copy-start | bytes 2308

commit v2 on v1

--- a/solution.py
+++ b/solution.py
@@ -603,10 +603,10 @@
 
 
 def attend_back_kernel(
-    n, q_ref, k_ref, v_ref, lo_ref, lse_ref, of_ref, norm_ref, g_ref, gout, gud, side, part_sum,
+    n, q_ref, k_ref, v_ref, lo_ref, lse_ref, of_ref, norm, g_ref, gout, gud, side, part_sum,
     dall, gw_sum, zsum, osum, ssum,
-    qs, ks, vs, grow, qrow, delta, dqs, soft, dscore, dbuf, gw, gwx, gwr, zr, gud_v, obuf, ogot, sgot, stot, sdp, ssem, rsem, lsem,
-    zsend, zrecv, xsend, xrecv, osend, orecv, olocal, vlocal, s_send, s_recv, s_local, dsend, drecv,
+    qs, ks, vs, grow, qrow, delta, dqs, soft, dscore, norm_v, dbuf, gw, gwx, gwr, zr, gud_v, obuf, ogot, sgot, stot, sdp, ssem, rsem, lsem,
+    zsend, zrecv, xsend, xrecv, osend, orecv, olocal, vlocal, nlocal, s_send, s_recv, s_local, dsend, drecv,
 ):
     u = pl.program_id(0)
     c, t = place()
@@ -694,11 +694,16 @@
             return pltpu.make_async_copy(gud, gud_v, vlocal.at[2])
         return pltpu.make_async_copy(part_sum.at[i], zr.at[0, i, 0], vlocal.at[i])
 
+    def normed(i):
+        return pltpu.make_async_copy(norm.at[i], norm_v.at[i], nlocal.at[i])
+
     @pl.when(u == 0)
     def _():
         greet(peers)
         for i in range(3):
             load(i).start()
+        for i in range(2):
+            normed(i).start()
         gw[...] = jnp.zeros_like(gw)
         greeted(peers)
         out_grad(4).start()
@@ -780,13 +785,19 @@
             src, dst, ssem.at[i - 1, unit], rsem.at[i - 1, unit], device_id=at_peer(c, t, dc, r)
         )
 
+    for i, at in enumerate((0, 3)):
+
+        @pl.when(u == at)
+        def _():
+            normed(i).wait()
+
     @pl.when(sends(u, c))
     def _():
         for i in range(1, len(PEERS)):
             move(u, i, c).start()
         move(u, 0, c).start()
         h, _ = unit_place(u, c)
-        gw[h] += nn(dbuf[u].reshape(3 * HD, length), norm_ref[0])
+        gw[h] += nn(dbuf[u].reshape(3 * HD, length), norm_v[u // 3])
 
     @pl.when(u == pl.num_programs(0) - 1)
     def _():
@@ -848,7 +859,7 @@
             pl.BlockSpec((1, 1, length), lambda u: (u // 3, 0, 0)),
             unit(1, length),
             unit(HD, length),
-            pl.BlockSpec((1, length, width), lambda u: (u // 3, 0, 0)),
+            HBM,
             unit(HD, length),
             once(grad_out.shape),
         ]
@@ -857,14 +868,14 @@
         scratch_shapes=[
             wide, tall, tall, tall, tall,
             pltpu.VMEM((1, length), full), pltpu.VMEM((HD, length), full),
-            pltpu.VMEM((QB, WIN + QB), low), pltpu.VMEM((QB, WIN + QB), low),
+            pltpu.VMEM((QB, WIN + QB), low), pltpu.VMEM((QB, WIN + QB), low), pltpu.VMEM(normed.shape, low),
             pltpu.VMEM((UNITS, 3, HD, length), low), pltpu.VMEM((3, 3 * HD, width), full),
             pltpu.VMEM((2, width, 6 * HD), low), pltpu.VMEM((width, 6 * HD), low),
             pltpu.VMEM((2, 2, n - 1, 2, shard, columns), low), pltpu.VMEM(grad_up_down.shape, low),
             pltpu.VMEM((4, local, out_rows), low), pltpu.VMEM((4, local, out_rows), low),
             pltpu.VMEM((4, width, SIDE), low), pltpu.VMEM((width, SIDE), low), pltpu.VMEM((n - 1, shard, SIDE), low),
             dma((7, UNITS)), dma((7, UNITS)), dma((UNITS,)),
-            dma((2, 2, n - 1)), dma((2, 2, n - 1)), dma, dma, dma((4,)), dma((4,)), dma, dma((3,)),
+            dma((2, 2, n - 1)), dma((2, 2, n - 1)), dma, dma, dma((4,)), dma((4,)), dma, dma((3,)), dma((2,)),
             dma((3,)), dma((3,)), dma, dma((n - 1,)), dma((n - 1,)),
         ],
         out_shape=[shape((4, 3, 3, HD, 3 * own), low)]
@@ -1149,10 +1160,11 @@
 
 
 def feed_kernel(
-    dp, att, proj, tokens, cot, gains, w_t, up_ref, down_ref,
-    result, middle, gout, gud, side, part_sum, units, w_all,
+    dp, att_ref, proj_ref, tokens_ref, cot_ref, gains, w_t_ref, up_ref, down_ref,
+    result, grad_middle, gout, gud, side, part_sum, units, w_all,
     x, g, x_t, g_t, up, down, act, gh, out, back, proj_w, sent, got, gbuf, sbuf, gatt,
-    xsend, xrecv, wsend, wrecv, wlocal, zsend, zrecv, glocal, usend, urecv, ulocal, load,
+    att, proj, tokens, cot, w_t, middle,
+    xsend, xrecv, wsend, wrecv, wlocal, zsend, zrecv, glocal, usend, urecv, ulocal, load, first_load, mlocal,
 ):
     c, t = place()
     d = lax.axis_index("dp")
@@ -1226,15 +1238,26 @@
     ]
     greet(peers)
     greet_line(dp, d)
-    for copy in loads:
+    firsts = [
+        pltpu.make_async_copy(src, dst, first_load.at[i])
+        for i, (src, dst) in enumerate(
+            ((cot_ref, cot), (proj_ref, proj), (w_t_ref, w_t), (att_ref, att), (tokens_ref, tokens))
+        )
+    ]
+    for copy in firsts + loads:
         copy.start()
+    for copy in firsts[:2]:
+        copy.wait()
     for p in range(4):
         proj_w[:, p * local : (p + 1) * local] = proj[p]
+    firsts[2].wait()
     greeted_line(dp, d, peers)
     cross(0).start()
     for r in range(1, 4):
         over_tensor(r).start()
     over_tensor(0).start()
+    for copy in firsts[3:]:
+        copy.wait()
     for m in range(0, rows, block):
         part = slice(m, m + block)
         v = tokens[part, :].astype(full) + nn(proj_w[...], att[:, part]).T
@@ -1314,6 +1337,8 @@
         for i in range(1, len(PEERS)):
             leave(whole, i).start()
         leave(whole, 0).start()
+    keep_middle = pltpu.make_async_copy(back, grad_middle, mlocal)
+    keep_middle.start()
 
     def weight_grad(j, a, left_t, right):
         @pl.loop(0, 3)
@@ -1343,7 +1368,7 @@
         gout[p] = nn(att[p * local : (p + 1) * local, :], x[mine, :]).astype(low)
     cross(3).wait_recv()
     result[...] = (middle[...] + out[...] + got[1].astype(full)).astype(low)
-    middle[...] = back[...]
+    keep_middle.wait()
     for k in (0, 2, 3):
         cross(k).wait_send()
     for r in range(1, 4):
@@ -1365,8 +1390,8 @@
     assert pieces == 4 and dp > 2 and rows == width
     return pl.pallas_call(
         functools.partial(feed_kernel, dp),
-        in_specs=[VMEM] * 6 + [HBM] * 2,
-        out_specs=[VMEM] * 3 + [HBM] * 5,
+        in_specs=[HBM] * 4 + [VMEM] + [HBM] * 3,
+        out_specs=[VMEM, HBM, VMEM] + [HBM] * 5,
         out_shape=[
             shape((rows, width), low),
             shape((rows, width), full),
@@ -1386,8 +1411,10 @@
         + [pltpu.VMEM((2, rows, width), low)] * 2
         + [pltpu.VMEM((2, 2, width, 2 * n - SIDE), low), pltpu.VMEM((4, width, SIDE), low)]
         + [pltpu.VMEM((12, HD, rows), low)]
+        + [pltpu.VMEM(a.shape, low) for a in (att, proj, tokens, cot, w_t)]
+        + [pltpu.VMEM((rows, width), full)]
         + [dma((4,)), dma((4,)), dma((4,)), dma((4,)), dma]
-        + [dma((2, 1)), dma((2, 1)), dma((3,)), dma((2, 7)), dma((2, 7)), dma((2,)), dma((2, 4))],
+        + [dma((2, 1)), dma((2, 1)), dma((3,)), dma((2, 7)), dma((2, 7)), dma((2,)), dma((2, 4)), dma((5,)), dma],
         compiler_params=pltpu.CompilerParams(
             vmem_limit_bytes=63 << 20, collective_id=5, has_side_effects=True
         ),

time: 251 us -> 248 us (0.988)
  Pallas kernels: 246 us -> 243 us
    pallas_call x1, Pallas kernels: 48.2 us -> 45.4 us  [feed(): pl.pallas_call(functools.partial(feed_kernel, dp), in_specs=[HBM] * 4 + [...]
where the time goes in v2:
time: 248 us
  Pallas kernels  243 us (98%)
  local copies, waits for them, and re-layouts  3.58 us (1%)
    pallas_call x1, Pallas kernels, attend_back(): pl.pallas_call(functools.partial(attend_back_kernel, n), grid=(UNITS,), i...  63.6 us
    pallas_call x1, Pallas kernels, attend(): pl.pallas_call(functools.partial(attend_kernel, n), grid=(UNITS,), in_spe...  53.4 us
    pallas_call x1, Pallas kernels, project(): pl.pallas_call(functools.partial(project_kernel, n), in_specs=[HBM, VMEM,...  51.5 us
    pallas_call x1, Pallas kernels, feed(): pl.pallas_call(functools.partial(feed_kernel, dp), in_specs=[HBM] * 4 + [...  45.4 us
    pallas_call x1, Pallas kernels, last(): pl.pallas_call(functools.partial(last_kernel, n), in_specs=[HBM] * 4 + [V...  25.5 us

profile of v2, /device:TPU:1, one launch (start us, length us, event | category | flops | bytes accessed | tf_op | source)
XLA Modules:
  0.0 247.5 jit_solution(6314233660069933519)
XLA Ops:
  0.6 1.2 reshape.46.gain_one
  1.9 1.2 reshape.47.gain_two
  3.1 51.5 %project.1 = (bf16[15,64,2048]{2,1,0:T(8,128)(2,1)}, bf16[2,2048,768]{2,1,0:T(8,128)(2,1)}, bf16[576,768]{1,0:T(8,128)(2,1)}, bf16[768,384]{1,0:T(8,128)(2,1)}, ...) custom-call(bf16[3,256,768]{2,1,0:T(8,128)(2,1)} %tokens.1, s32[3,2048]{1,0:T(4,128)} %segments.1, ...), custom_call_target="tpu_custom_call" | custom-call | tf_op jit(solution)/shard_map/project/pallas_call | solution.py:328
  54.6 53.4 %attend.1 = (bf16[768,768]{1,0:T(8,128)(2,1)}, f32[5,1,2048]{2,1,0:T(1,128)}, f32[5,64,2048]{2,1,0:T(8,128)}, bf16[4,768,384]{2,1,0:T(8,128)(2,1)}, bf16[4,768,3...) custom-call(bf16[15,64,2048]{2,1,0:T(8,128)(2,1)} %get-tuple-element.47.q_ref.k_ref.v_ref, ...), custom_call_target="tpu_custom_call" | custom-call | flops 6039797760 | bytes 20971520 | tf_op jit(solution)/shard_map/attend/pallas_call | solution.py:556
  108.1 45.4 %feed.1 = (bf16[768,768]{1,0:T(8,128)(2,1)}, f32[768,768]{1,0:T(8,128)}, bf16[4,192,768]{2,1,0:T(8,128)(2,1)}, bf16[4,768,640]{2,1,0:T(8,128)(2,1)}, bf16[4,768,...) custom-call(bf16[768,768]{1,0:T(8,128)(2,1)} %get-tuple-element.51.a, ...), custom_call_target="tpu_custom_call" | custom-call | tf_op jit(solution)/shard_map/feed/pallas_call | solution.py:1391
  153.5 63.6 %attend_back.1 = (bf16[4,3,3,64,768]{4,3,2,1,0:T(8,128)(2,1)}, bf16[768,384]{1,0:T(8,128)(2,1)}, bf16[4,192,640]{2,1,0:T(8,128)(2,1)}, bf16[384,192]{1,0:T(8,128)(2,1)}, f32[192,128]{1,0:T(8,128)}) custom-call(bf16[15,64,2048]{2,1,0:T(8,128)(2,1)} %get-tuple-element.47.q_ref.k_ref.v_ref, bf16[15,64,2048]{2,1,0:T(8,128)(2,1)} %get-tuple-element.47.q_ref.k_ref.v_ref, ...), custom_call_target="tpu_custom_call" | custom-call | tf_op jit(solution)/shard_map/attend_back/pallas_call | solution.py:854
  217.2 25.5 %last.1 = (bf16[768,768]{1,0:T(8,128)(2,1)}, f32[192,768]{1,0:T(8,128)}, f32[192,768]{1,0:T(8,128)}, f32[192,768]{1,0:T(8,128)}, f32[192,192]{1,0:T(8,128)}, /*index=5*/f32[1,192]{1,0:T(1,128)}, f32[1,192]{1,0:T(1,128)}) custom-call(bf16[2304,768]{1,0:T(8,128)(2,1)} %bitcast.15, bf16[2304,768]{1,0:T(8,128)(2,1)} %bitcast.14, bf16[768,768]{1,0:T(8,128)(2,1)} %bitcast.13, ...), custom_call_target="tpu_custom_call" | custom-call | tf_op jit(solution)/shard_map/last/pallas_call | solution.py:1091
  242.7 0.0 copy-start.1
  242.7 0.0 copy-start
  242.7 3.7 %close.1 = (bf16[768,768]{1,0:T(8,128)(2,1)}, bf16[768,768]{1,0:T(8,128)(2,1)}, f32[3,192,192]{2,1,0:T(8,128)}, f32[192,192]{1,0:T(8,128)}, f32[192,768]{1,0:T(8,128)}, /*index=5*/f32[192,768]{1,0:T(8,128)}) custom-call(bf16[768,768]{1,0:T(8,128)(2,1)} %get-tuple-element.57.refs_0_, bf16[768,768]{1,0:T(8,128)(2,1)} %get-tuple-element.73.refs_1_, ...), custom_call_target="tpu_custom_call" | custom-call | tf_op jit(solution)/shard_map/close/pallas_call | solution.py:1142
  246.4 0.0 copy-done.1
  246.4 0.6 copy.19
  247.0 0.0 copy-done
  247.0 0.6 copy.20
Async XLA Ops:
  242.7 3.7 %copy-start.1 = (f32[1,192]{1,0:T(1,128)S(1)}, f32[1,192]{1,0:T(1,128)}, u32[]{:S(2)}) copy-start(f32[1,192]{1,0:T(1,128)} %get-tuple-element.84) | copy-start | bytes 2308
  242.7 4.3 %copy-start = (f32[1,192]{1,0:T(1,128)S(1)}, f32[1,192]{1,0:T(1,128)}, u32[]{:S(2)}) copy-start(f32[1,192]{1,0:T(1,128)} %get-tuple-element.85) | copy-start | bytes 2308

commit v3 on v2

--- a/solution.py
+++ b/solution.py
@@ -1122,29 +1122,41 @@
 
 
 def close_kernel(*refs):
-    count = len(refs) // 2
-    for i, (src, dst) in enumerate(zip(refs[:count], refs[count:])):
+    count = (len(refs) - 3) // 3
+    sources, targets, held = refs[:count], refs[count : 2 * count], refs[2 * count : 3 * count]
+    parts, into, out = refs[3 * count :]
+    loads = [
+        pltpu.make_async_copy(src, dst, into.at[i]) for i, (src, dst) in enumerate(zip(sources, held))
+    ]
+    stores = [
+        pltpu.make_async_copy(parts if i == 2 else src, dst, out.at[i])
+        for i, (src, dst) in enumerate(zip(held, targets))
+    ]
+    for copy in loads:
+        copy.start()
+    local = parts.shape[2]
+    for i in range(count):
+        loads[i].wait()
         if i == 2:
-            local = dst.shape[2]
             for p in range(3):
-                dst[p] = src[:, p * local : (p + 1) * local]
-        else:
-            dst[...] = src[...]
+                parts[p] = held[2][:, p * local : (p + 1) * local]
+        stores[i].start()
+    for copy in stores:
+        copy.wait()
 
 
 def close(result, grad_input, own_attn, *others):
     arrays = (result, grad_input, own_attn, *others)
-    rows = lambda a: pl.BlockSpec((a.shape[0] // 2, a.shape[1]), lambda i: (i, 0))
     shard, local = own_attn.shape[0], others[0].shape[0]
-    parts = pl.BlockSpec((3, shard // 2, local), lambda i: (0, i, 0))
     outs = [shape(a.shape, a.dtype) for a in arrays]
     outs[2] = shape((3, shard, local), full)
     return pl.pallas_call(
         close_kernel,
-        grid=(2,),
-        in_specs=[rows(a) for a in arrays],
-        out_specs=[parts if i == 2 else rows(a) for i, a in enumerate(arrays)],
+        in_specs=[HBM] * len(arrays),
+        out_specs=[HBM] * len(arrays),
         out_shape=outs,
+        scratch_shapes=[pltpu.VMEM(a.shape, a.dtype) for a in arrays]
+        + [pltpu.VMEM((3, shard, local), full), dma((len(arrays),)), dma((len(arrays),))],
         compiler_params=pltpu.CompilerParams(vmem_limit_bytes=63 << 20),
         name="close",
     )(*arrays)

time: 248 us -> 248 us (level)
  no operation moved by 1% of the time
where the time goes in v3:
time: 248 us; the launch traced here: 247 us
  Pallas kernels  243 us (98%)
  local copies, waits for them, and re-layouts  3.58 us (1%)
    pallas_call x1, Pallas kernels, attend_back(): pl.pallas_call(functools.partial(attend_back_kernel, n), grid=(UNITS,), i...  63.6 us
    pallas_call x1, Pallas kernels, attend(): pl.pallas_call(functools.partial(attend_kernel, n), grid=(UNITS,), in_spe...  53.4 us
    pallas_call x1, Pallas kernels, project(): pl.pallas_call(functools.partial(project_kernel, n), in_specs=[HBM, VMEM,...  51.5 us
    pallas_call x1, Pallas kernels, feed(): pl.pallas_call(functools.partial(feed_kernel, dp), in_specs=[HBM] * 4 + [...  45.4 us
    pallas_call x1, Pallas kernels, last(): pl.pallas_call(functools.partial(last_kernel, n), in_specs=[HBM] * 4 + [V...  25.5 us

profile of v3, /device:TPU:1, one launch (start us, length us, event | category | flops | bytes accessed | tf_op | source)
XLA Modules:
  0.0 247.3 jit_solution(7889173293064654418)
XLA Ops:
  0.6 1.2 reshape.46.gain_one
  1.9 1.2 reshape.47.gain_two
  3.1 51.5 %project.1 = (bf16[15,64,2048]{2,1,0:T(8,128)(2,1)}, bf16[2,2048,768]{2,1,0:T(8,128)(2,1)}, bf16[576,768]{1,0:T(8,128)(2,1)}, bf16[768,384]{1,0:T(8,128)(2,1)}, ...) custom-call(bf16[3,256,768]{2,1,0:T(8,128)(2,1)} %tokens.1, s32[3,2048]{1,0:T(4,128)} %segments.1, ...), custom_call_target="tpu_custom_call" | custom-call | tf_op jit(solution)/shard_map/project/pallas_call | solution.py:328
  54.6 53.4 %attend.1 = (bf16[768,768]{1,0:T(8,128)(2,1)}, f32[5,1,2048]{2,1,0:T(1,128)}, f32[5,64,2048]{2,1,0:T(8,128)}, bf16[4,768,384]{2,1,0:T(8,128)(2,1)}, bf16[4,768,3...) custom-call(bf16[15,64,2048]{2,1,0:T(8,128)(2,1)} %get-tuple-element.47.q_ref.k_ref.v_ref, ...), custom_call_target="tpu_custom_call" | custom-call | flops 6039797760 | bytes 20971520 | tf_op jit(solution)/shard_map/attend/pallas_call | solution.py:556
  108.1 45.4 %feed.1 = (bf16[768,768]{1,0:T(8,128)(2,1)}, f32[768,768]{1,0:T(8,128)}, bf16[4,192,768]{2,1,0:T(8,128)(2,1)}, bf16[4,768,640]{2,1,0:T(8,128)(2,1)}, bf16[4,768,...) custom-call(bf16[768,768]{1,0:T(8,128)(2,1)} %get-tuple-element.51.a, ...), custom_call_target="tpu_custom_call" | custom-call | tf_op jit(solution)/shard_map/feed/pallas_call | solution.py:1403
  153.5 63.6 %attend_back.1 = (bf16[4,3,3,64,768]{4,3,2,1,0:T(8,128)(2,1)}, bf16[768,384]{1,0:T(8,128)(2,1)}, bf16[4,192,640]{2,1,0:T(8,128)(2,1)}, bf16[384,192]{1,0:T(8,128)(2,1)}, f32[192,128]{1,0:T(8,128)}) custom-call(bf16[15,64,2048]{2,1,0:T(8,128)(2,1)} %get-tuple-element.47.q_ref.k_ref.v_ref, bf16[15,64,2048]{2,1,0:T(8,128)(2,1)} %get-tuple-element.47.q_ref.k_ref.v_ref, ...), custom_call_target="tpu_custom_call" | custom-call | tf_op jit(solution)/shard_map/attend_back/pallas_call | solution.py:854
  217.2 25.5 %last.1 = (bf16[768,768]{1,0:T(8,128)(2,1)}, f32[192,768]{1,0:T(8,128)}, f32[192,768]{1,0:T(8,128)}, f32[192,768]{1,0:T(8,128)}, f32[192,192]{1,0:T(8,128)}, /*index=5*/f32[1,192]{1,0:T(1,128)}, f32[1,192]{1,0:T(1,128)}) custom-call(bf16[2304,768]{1,0:T(8,128)(2,1)} %bitcast.15, bf16[2304,768]{1,0:T(8,128)(2,1)} %bitcast.14, bf16[768,768]{1,0:T(8,128)(2,1)} %bitcast.13, ...), custom_call_target="tpu_custom_call" | custom-call | tf_op jit(solution)/shard_map/last/pallas_call | solution.py:1091
  242.7 0.0 copy-start.1
  242.7 0.0 copy-start
  242.7 3.4 %close.1 = (bf16[768,768]{1,0:T(8,128)(2,1)}, bf16[768,768]{1,0:T(8,128)(2,1)}, f32[3,192,192]{2,1,0:T(8,128)}, f32[192,192]{1,0:T(8,128)}, f32[192,768]{1,0:T(8,128)}, /*index=5*/f32[192,768]{1,0:T(8,128)}) custom-call(bf16[768,768]{1,0:T(8,128)(2,1)} %get-tuple-element.57.refs_0_, bf16[768,768]{1,0:T(8,128)(2,1)} %get-tuple-element.73.refs_1_, ...), custom_call_target="tpu_custom_call" | custom-call | tf_op jit(solution)/shard_map/close/pallas_call | solution.py:1153
  246.1 0.0 copy-done.1
  246.2 0.6 copy.19
  246.7 0.0 copy-done
  246.7 0.6 copy.20
Async XLA Ops:
  242.7 3.5 %copy-start.1 = (f32[1,192]{1,0:T(1,128)S(1)}, f32[1,192]{1,0:T(1,128)}, u32[]{:S(2)}) copy-start(f32[1,192]{1,0:T(1,128)} %get-tuple-element.84) | copy-start | bytes 2308
  242.7 4.0 %copy-start = (f32[1,192]{1,0:T(1,128)S(1)}, f32[1,192]{1,0:T(1,128)}, u32[]{:S(2)}) copy-start(f32[1,192]{1,0:T(1,128)} %get-tuple-element.85) | copy-start | bytes 2308
